TPU v7x, 512 devices: a whole 4x8x8 slice. The times are simulated.
512 devices in a mesh: rows: 32 (over x, z), cols: 16 (over y, core).
Axes of the slice: x: 4, y: 8, z: 8, core: 2. Of those that a mesh axis runs over, the one named last changes fastest.
Arguments:
- points: float32 [3, 131072], P(None, 'rows'), as said below
- targets: float32 [16, 131072], P(None, 'rows'), may hold values from -6 to 6
- landmarks: int32 [256], replicated, may hold values from 0 to 131071
- neighbours: int32 [1024, 18], P('rows'), may hold values from 0 to 1023, as said below
- counts: int32 [1024], P('rows'), may hold values from 1 to 18
- core_inverse: float32 [256, 256], replicated, as said below
Outputs:
- solution: float32 [16, 131072], P(None, 'rows')
- residual: float32 [16, 131072], P(None, 'rows')
Inputs may be any that keep to these rules, and one draw needn't show every extreme that they name: `neighbours`: for block b the first counts[b] entries are distinct blocks in ascending order, b among them, each within 12 blocks of b; b lists c exactly when c lists b; the remaining slots hold b. `points`: points of blocks that do not list each other are farther apart than 1. `core_inverse`: Symmetric; each diagonal entry exceeds the sum of the magnitudes of the other entries of its row.
All inputs are finite; a program needn't handle non-finite values.
Results may differ from a plain program's by a relative error of at most 0.0003.
Values sent between devices are 32-bit elements; how exact they have to be, the bound alone decides.
A program may use at most 64 MiB of HBM per device.

v0:
```python
import jax
import jax.numpy as jnp
from jax import lax
from jax.sharding import PartitionSpec as P

MOST = 6
ITERS = 2
kernel_scale = 0.03125
ridge_shift = 1.0
tile_group = 32


def extended(cells, sides, width):
    for axis, dim in sides:
        count = lax.axis_size(axis)
        ends = count - 1
        head = lax.slice_in_dim(cells, 0, width, axis=dim)
        tail = lax.slice_in_dim(cells, cells.shape[dim] - width, cells.shape[dim], axis=dim)
        cells = jnp.concatenate(
            [
                lax.ppermute(tail, axis, [(i, (i + 1) % count) for i in range(ends)]),
                cells,
                lax.ppermute(head, axis, [((i + 1) % count, i) for i in range(ends)]),
            ],
            axis=dim,
        )
    return cells


def wendland(squared):
    distance = jnp.sqrt(squared)
    remain = jnp.maximum(1.0 - distance, 0.0)
    return remain * remain * remain * remain * (4.0 * distance + 1.0)


def squared_gap(first_pts, second_pts):
    offsets = first_pts[:, :, None] - second_pts[:, None, :]
    return jnp.sum(offsets * offsets, axis=0)


def tile_products(vector_halo, point_halo, row_points, nearby, amounts, last_tile):
    block_count = row_points.shape[1]
    block_width = row_points.shape[2]
    slot_count = nearby.shape[1]
    tile_ends = jnp.cumsum(amounts)
    tile_starts = tile_ends - amounts
    lane_ids = jnp.arange(tile_group, dtype=jnp.int32)
    block_ids = jnp.arange(block_count, dtype=jnp.int32)
    turn_count = (last_tile + tile_group - 1) // tile_group

    def advance(turn_index, running):
        position = turn_index * tile_group + lane_ids
        inside = position < last_tile
        owner_block = jnp.sum((tile_ends[None, :] <= position[:, None]).astype(jnp.int32), axis=1)
        owner_block = jnp.minimum(owner_block, block_count - 1)
        column = jnp.clip(position - tile_starts[owner_block], 0, slot_count - 1)
        partner = nearby[owner_block, column]
        row_side = row_points[:, owner_block]
        col_side = point_halo[:, partner]
        offsets = row_side[:, :, :, None] - col_side[:, :, None, :]
        kernel_tiles = wendland(jnp.sum(offsets * offsets, axis=0)) * inside[:, None, None].astype(
            jnp.float32
        )
        contrib = jnp.einsum(
            "ogn,gmn->ogm", vector_halo[:, partner], kernel_tiles, precision=lax.Precision.HIGHEST
        )
        placing = ((owner_block[:, None] == block_ids[None, :]) & inside[:, None]).astype(
            jnp.float32
        )
        return running + jnp.einsum(
            "ogm,gb->obm", contrib, placing, precision=lax.Precision.HIGHEST
        )

    start_total = jnp.zeros((vector_halo.shape[0], block_count, block_width), jnp.float32)
    return lax.fori_loop(0, turn_count, advance, start_total)


def body(points, targets, landmarks, neighbours, counts, core_inverse):
    col_count = lax.axis_size("cols")
    row_index = lax.axis_index("rows")
    col_index = lax.axis_index("cols")
    block_count = neighbours.shape[0]
    slab_points = points.shape[1]
    block_width = slab_points // block_count
    share_blocks = block_count // col_count
    share_points = share_blocks * block_width
    outputs_count = targets.shape[0]
    reach = 2 * MOST
    first_block = row_index * block_count
    local_ids = landmarks - row_index * slab_points
    present = (local_ids >= 0) & (local_ids < slab_points)
    picked = jnp.take(points, jnp.clip(local_ids, 0, slab_points - 1), axis=1) * present[
        None, :
    ].astype(jnp.float32)
    landmark_coords = lax.psum(picked, "rows")
    share_start = col_index * share_points
    own_points = lax.dynamic_slice_in_dim(points, share_start, share_points, 1)
    landmark_kernel = kernel_scale * wendland(squared_gap(landmark_coords, own_points))

    def precondition_share(residual_share):
        projected = jnp.dot(residual_share, landmark_kernel.T, precision=lax.Precision.HIGHEST)
        projected = lax.psum(projected, ("rows", "cols"))
        weights = jnp.dot(projected, core_inverse, precision=lax.Precision.HIGHEST)
        shared = residual_share - jnp.dot(weights, landmark_kernel, precision=lax.Precision.HIGHEST)
        product = lax.psum(jnp.sum(residual_share * shared, axis=1), ("rows", "cols"))
        return (shared, product)

    point_halo = extended(points, (("rows", 1),), reach * block_width)
    point_halo = point_halo.reshape(3, -1, block_width)
    nearby = neighbours - (first_block - reach)

    def share_of(vector):
        return lax.dynamic_slice_in_dim(vector, share_start, share_points, 1)

    def precondition(residual):
        shared, product = precondition_share(share_of(residual))
        return (lax.all_gather(shared, "cols", axis=1, tiled=True), product)

    solution = jnp.zeros_like(targets)
    residual = targets
    preconditioned, current = precondition(residual)
    direction = preconditioned
    for iteration in range(ITERS):
        vector_halo = extended(direction, (("rows", 1),), reach * block_width)
        vector_halo = vector_halo.reshape(outputs_count, -1, block_width)
        own_lists = lax.dynamic_slice_in_dim(nearby, col_index * share_blocks, share_blocks, 0)
        amounts = lax.dynamic_slice_in_dim(counts, col_index * share_blocks, share_blocks, 0)
        rows_here = own_points.reshape(3, share_blocks, block_width)
        tile_total = jnp.sum(amounts)
        partial_rows = tile_products(
            vector_halo, point_halo, rows_here, own_lists, amounts, tile_total
        )
        operate_product = lax.all_gather(
            partial_rows.reshape(outputs_count, share_points), "cols", axis=1, tiled=True
        )
        applied = kernel_scale * operate_product + ridge_shift * direction
        curvature_part = jnp.sum(share_of(direction) * share_of(applied), axis=1)
        step_size = current / lax.psum(curvature_part, ("rows", "cols"))
        solution = solution + step_size[:, None] * direction
        residual = residual - step_size[:, None] * applied
        if iteration + 1 < ITERS:
            preconditioned, following = precondition(residual)
            direction = preconditioned + (following / current)[:, None] * direction
            current = following
    solution, residual = (solution, residual)
    return (solution, residual)


def solution(mesh):
    placed = (P(None, "rows"), P(None, "rows"), P(), P("rows", None), P("rows"), P())
    return jax.shard_map(
        body,
        mesh=mesh,
        in_specs=placed,
        out_specs=(P(None, "rows"), P(None, "rows")),
        check_vma=False,
    )
```

profile of v0, /device:TPU:1, one launch (start us, length us, event | category | flops | bytes accessed | tf_op | source)
XLA Modules:
  0.0 767.7 jit_solution(12587315131149481955)
XLA Ops:
  0.7 0.8 fusion.98
  1.5 4.8 collective-permute-start
  6.3 1.3 collective-permute-start.1
  7.6 1.5 copy.37
  9.2 0.7 gather_fusion.8
  10.1 121.2 %psum.49 = f32[3,256]{0,1:T(8,128)S(1)} all-reduce(f32[3,256]{0,1:T(8,128)S(1)} %multiply_bitcast_fusion), channel_id=1, replica_groups=mesh['rows'=32,'cols'=16] {'rows'}, use_global_device_ids=true, to_apply=%region_0.1 | all-reduce | flops 768 | bytes 6144 | tf_op jit(solution)/shard_map/psum | solution.py:95
  131.6 0.4 fusion.84
  132.0 124.0 %psum.50 = f32[16,256]{1,0:T(8,128)S(1)} all-reduce(f32[16,256]{1,0:T(8,128)S(1)} %fusion.84), channel_id=1, replica_groups=mesh['rows'=32,'cols'=16] {'rows','cols'}, use_global_device_ids=true, to_apply=%region_2.3 | all-reduce | flops 4096 | bytes 32768 | tf_op jit(solution)/shard_map/psum | solution.py:102
  256.2 0.5 multiply_reduce_fusion.6
  256.7 16.2 %all_gather.12 = f32[16,4096]{1,0:T(8,128)S(1)} all-gather(f32[16,256]{1,0:T(8,128)S(1)} %get-tuple-element.306), channel_id=1, replica_groups=mesh['rows'=32,'cols'=16] {'cols'}, dimensions={1}, use_global_device_ids=true | all-gather | bytes 278528 | tf_op jit(solution)/shard_map/all_gather | solution.py:117
  272.9 2.8 collective-permute-start.2
  275.7 1.3 collective-permute-start.3
  277.3 0.8 bitcast_subtract_fusion
  279.0 2.5 collective-permute-done.3
  281.6 12.1 %while.22 = (s32[]{:T(128)}, f32[16,2,128]{2,1,0:T(2,128)S(1)}, s32[]{:T(128)}, s32[2]{0:T(128)S(1)}, s32[]{:T(128)}, /*index=5*/f32[3,2,128]{2,0,1:T(4,128)S(1)...) while((s32[]{:T(128)}, f32[16,2,128]{2,1,0:T(2,128)S(1)}, ...), condition=%wide.region_10.11_spmd.clone, body=%wide.region_7.10_spmd.clone.sunk | while | flops 111156288 | bytes 6040561 | solution.py:75
  281.7 0.6 fusion.135
  282.3 1.3 fusion.136
  283.6 0.8 gather_fusion
  284.4 0.7 fusion.138
  285.1 0.6 gather_fusion.2
  285.7 0.6 gather_fusion.1
  286.4 0.6 gather_fusion.3
  287.0 2.1 multiply_reduce_fusion.9
  289.0 4.3 fusion.139
  293.7 16.3 %all_gather.13 = f32[16,4096]{1,0:T(8,128)S(1)} all-gather(f32[16,256]{1,0:T(8,128)S(1)} %bitcast.164), channel_id=1, replica_groups=mesh['rows'=32,'cols'=16] {'cols'}, dimensions={1}, use_global_device_ids=true | all-gather | bytes 278528 | tf_op jit(solution)/shard_map/all_gather | solution.py:133
  310.1 104.1 %all-reduce = (f32[16]{0:T(128)S(1)}, f32[16]{0:T(128)S(1)}) all-reduce(f32[16]{0:T(128)S(1)} %get-tuple-element.305, f32[16]{0:T(128)S(1)} %multiply_reduce_fusion.5), channel_id=1, replica_groups=mesh['rows'=32,'cols'=16] {'rows','cols'}, use_global_device_ids=true, to_apply=%region_4.5 | all-reduce | flops 32 | bytes 256 | tf_op jit(solution)/shard_map/psum | solution.py:105
  414.3 0.4 fusion.82
  414.7 94.7 %psum.53 = f32[16,256]{1,0:T(8,128)S(1)} all-reduce(f32[16,256]{1,0:T(8,128)S(1)} %fusion.82), channel_id=1, replica_groups=mesh['rows'=32,'cols'=16] {'rows','cols'}, use_global_device_ids=true, to_apply=%region_13.14 | all-reduce | flops 4096 | bytes 32768 | tf_op jit(solution)/shard_map/psum | solution.py:102
  509.6 0.5 multiply_reduce_fusion.4
  510.1 95.3 %psum.54 = f32[16]{0:T(128)S(1)} all-reduce(f32[16]{0:T(128)S(1)} %get-tuple-element.307), channel_id=1, replica_groups=mesh['rows'=32,'cols'=16] {'rows','cols'}, use_global_device_ids=true, to_apply=%region_15.16 | all-reduce | flops 16 | bytes 128 | tf_op jit(solution)/shard_map/psum | solution.py:105
  605.4 18.2 %all_gather.14 = f32[16,4096]{1,0:T(8,128)S(1)} all-gather(f32[16,256]{1,0:T(8,128)S(1)} %get-tuple-element.308), channel_id=1, replica_groups=mesh['rows'=32,'cols'=16] {'cols'}, dimensions={1}, use_global_device_ids=true | all-gather | bytes 278528 | tf_op jit(solution)/shard_map/all_gather | solution.py:117
  623.7 1.7 collective-permute-start.4
  625.4 1.3 collective-permute-start.5
  626.7 0.7 collective-permute-done.4
  627.4 4.6 collective-permute-done.5
  632.1 12.0 %while.23 = (s32[]{:T(128)}, f32[16,2,128]{2,1,0:T(2,128)S(1)}, s32[]{:T(128)}, s32[2]{0:T(128)S(1)}, s32[]{:T(128)}, /*index=5*/f32[3,2,128]{2,0,1:T(4,128)S(1)...) while((s32[]{:T(128)}, f32[16,2,128]{2,1,0:T(2,128)S(1)}, ...), condition=%wide.region_19.20_spmd.clone, body=%wide.region_16.19_spmd.clone.sunk | while | flops 111156288 | bytes 6040561 | solution.py:75
  632.2 0.6 fusion.146
  632.8 1.3 fusion.147
  634.1 0.8 gather_fusion.4
  634.8 0.7 fusion.149
  635.6 0.6 gather_fusion.6
  636.2 0.6 gather_fusion.5
  636.8 0.6 gather_fusion.7
  637.4 2.1 multiply_reduce_fusion.10
  639.5 4.3 fusion.150
  644.1 17.1 %all_gather.15 = f32[16,4096]{1,0:T(8,128)S(1)} all-gather(f32[16,256]{1,0:T(8,128)S(1)} %bitcast.165), channel_id=1, replica_groups=mesh['rows'=32,'cols'=16] {'cols'}, dimensions={1}, use_global_device_ids=true | all-gather | bytes 278528 | tf_op jit(solution)/shard_map/all_gather | solution.py:133
  661.4 105.4 %psum.55 = f32[16]{0:T(128)S(1)} all-reduce(f32[16]{0:T(128)S(1)} %multiply_reduce_fusion.3), channel_id=1, replica_groups=mesh['rows'=32,'cols'=16] {'rows','cols'}, use_global_device_ids=true, to_apply=%region_21.22 | all-reduce | flops 16 | bytes 128 | tf_op jit(solution)/shard_map/psum | solution.py:138
  766.8 0.9 multiply_subtract_fusion
  (64 shorter events, 2.8 us)
Async XLA Ops:
  0.6 255.4 %copy-start = (f32[256,256]{1,0:T(8,128)S(1)}, f32[256,256]{1,0:T(8,128)}, u32[]{:S(2)}) copy-start(f32[256,256]{1,0:T(8,128)} %param.15) | copy-start | bytes 786436
  0.6 8.5 %copy-start.1 = (f32[3,4096]{1,0:T(4,128)S(1)}, f32[3,4096]{1,0:T(4,128)}, u32[]{:S(2)}) copy-start(f32[3,4096]{1,0:T(4,128)} %param.10) | copy-start | bytes 147460
  0.7 8.5 %copy-start.4 = (s32[256]{0:T(256)S(1)}, s32[256]{0:T(256)}, u32[]{:S(2)}) copy-start(s32[256]{0:T(256)} %param.12) | copy-start | bytes 3076
  0.7 130.9 %copy-start.2 = (f32[16,4096]{1,0:T(8,128)S(1)}, f32[16,4096]{1,0:T(8,128)}, u32[]{:S(2)}) copy-start(f32[16,4096]{1,0:T(8,128)} %param.11) | copy-start | bytes 786436
  1.5 277.5 %collective-permute-start = (f32[3,1536]{1,0:T(4,128)S(1)}, f32[3,1536]{1,0:T(4,128)S(1)}, u32[]{:S(2)}, u32[]{:S(2)}) collective-permute-start(f32[3,1536]{1,0:T(4,128)S(1)} %get-tuple-element.298), channel_id=1, source_target_pairs={{0,16},{16,32},{32,48},{48,64},{64,80},{80,96},{96,112},{112,128},... | collective-permute-start | bytes 55304 | tf_op jit(solution)/shard_map/ppermute | solution.py:21
  6.3 272.6 %collective-permute-start.1 = (f32[3,1536]{1,0:T(4,128)S(1)}, f32[3,1536]{1,0:T(4,128)S(1)}, u32[]{:S(2)}, u32[]{:S(2)}) collective-permute-start(f32[3,1536]{1,0:T(4,128)S(1)} %get-tuple-element.299), channel_id=1, source_target_pairs={{16,0},{32,16},{48,32},{64,48},{80,64},{96,80},{112,96},{128,112},... | collective-permute-start | bytes 55304 | tf_op jit(solution)/shard_map/ppermute | solution.py:23
  9.1 267.9 %copy-start.5 = (s32[32]{0:T(128)S(1)}, s32[32]{0:T(128)}, u32[]{:S(2)}) copy-start(s32[32]{0:T(128)} %param.14) | copy-start | bytes 388
  9.1 269.0 %copy-start.3 = (s32[32,18]{0,1:T(8,128)S(1)}, s32[32,18]{0,1:T(8,128)}, u32[]{:S(2)}) copy-start(s32[32,18]{0,1:T(8,128)} %param.13) | copy-start | bytes 6916
  272.9 6.1 collective-permute-start.2
  275.7 5.8 collective-permute-start.3
  623.7 3.6 collective-permute-start.4
  625.4 6.6 collective-permute-start.5
where the time goes:
time: 769 us; the launch traced here: 768 us
  blocking collectives  713 us (93%)
  starting transfers between devices  13.1 us (2%)
  matrix products  11.3 us (1%)
  other arithmetic  11.2 us (1%)
  local copies, waits for them, and re-layouts  9.75 us (1%)
  waiting for transfers between devices  7.82 us (1%)
    psum x2, blocking collectives, precondition_share(): projected = lax.psum(projected, ('rows', 'cols'))  219 us
    psum x2, blocking collectives, precondition_share(): lax.psum(jnp.sum(residual_share * shared, axis=1), ('rows', 'cols'))  199 us
    psum x1, blocking collectives, body(): landmark_coords = lax.psum(picked, 'rows')  121 us
    psum x1, blocking collectives, body(): step_size = current / lax.psum(curvature_part, ('rows', 'cols'))  105 us
    all_gather x2, blocking collectives, precondition(): return (lax.all_gather(shared, 'cols', axis=1, tiled=True), product)  34.4 us
    all_gather x2, blocking collectives, body(): lax.all_gather(partial_rows.reshape(outputs_count, share_points), 'cols',...  33.5 us
  transfers between devices with their start and end apart: 6, of which 3 were waited for; matrix products, arithmetic and copies ran while one was open for 1% of the time, Pallas kernels for 0%

commit v1 on v0

--- a/solution.py
+++ b/solution.py
@@ -114,7 +114,12 @@
 
     def precondition(residual):
         shared, product = precondition_share(share_of(residual))
-        return (lax.all_gather(shared, "cols", axis=1, tiled=True), product)
+        return (
+            jnp.concatenate(
+                lax.all_to_all(jnp.stack([shared] * lax.axis_size("cols")), "cols", 0, 0), axis=1
+            ),
+            product,
+        )
 
     solution = jnp.zeros_like(targets)
     residual = targets

time: 769 us -> 762 us (level)
  blocking collectives: 713 us -> 682 us
  starting transfers between devices: 13.1 us -> 24.7 us
  waiting for transfers between devices: 7.82 us -> 19 us
    all_gather x2 -> x0, blocking collectives: 34.4 us -> none  [precondition(): return (lax.all_gather(shared, 'cols', axis=1, tiled=True), product)]
    all_to_all x0 -> x2, starting transfers between devices: none -> 10.2 us  [precondition(): lax.all_to_all(jnp.stack([shared] * lax.axis_size('cols')), 'cols', 0, 0)]
    all_to_all x0 -> x2, waiting for transfers between devices: none -> 9.64 us  [precondition(): lax.all_to_all(jnp.stack([shared] * lax.axis_size('cols')), 'cols', 0, 0)]
  transfers between devices with their start and end apart: 6 -> 8, of which waited for: 3 -> 5; matrix products, arithmetic and copies ran while one was open for 1% -> 1% of each run, Pallas kernels for 0% -> 0%
where the time goes in v1:
time: 762 us; the launch traced here: 761 us
  blocking collectives  682 us (90%)
  starting transfers between devices  24.7 us (3%)
  waiting for transfers between devices  19 us (2%)
  local copies, waits for them, and re-layouts  11.3 us (1%)
  matrix products  11.3 us (1%)
  other arithmetic  11.2 us (1%)
    psum x2, blocking collectives, precondition_share(): projected = lax.psum(projected, ('rows', 'cols'))  219 us
    psum x2, blocking collectives, precondition_share(): lax.psum(jnp.sum(residual_share * shared, axis=1), ('rows', 'cols'))  201 us
    psum x1, blocking collectives, body(): landmark_coords = lax.psum(picked, 'rows')  121 us
    psum x1, blocking collectives, body(): step_size = current / lax.psum(curvature_part, ('rows', 'cols'))  107 us
    all_gather x2, blocking collectives, body(): lax.all_gather(partial_rows.reshape(outputs_count, share_points), 'cols',...  33.2 us
  transfers between devices with their start and end apart: 8, of which 5 were waited for; matrix products, arithmetic and copies ran while one was open for 1% of the time, Pallas kernels for 0%

profile of v1, /device:TPU:1, one launch (start us, length us, event | category | flops | bytes accessed | tf_op | source)
XLA Modules:
  0.0 761.1 jit_solution(17470522865485707253)
XLA Ops:
  0.7 0.8 fusion.98
  1.5 4.8 collective-permute-start
  6.3 1.3 collective-permute-start.1
  7.6 1.5 copy.52
  9.2 0.7 gather_fusion.8
  10.1 121.2 %psum.49 = f32[3,256]{0,1:T(8,128)S(1)} all-reduce(f32[3,256]{0,1:T(8,128)S(1)} %multiply_bitcast_fusion), channel_id=1, replica_groups=mesh['rows'=32,'cols'=16] {'rows'}, use_global_device_ids=true, to_apply=%region_0.1 | all-reduce | flops 768 | bytes 6144 | tf_op jit(solution)/shard_map/psum | solution.py:95
  132.0 124.0 %psum.50 = f32[16,256]{1,0:T(8,128)S(1)} all-reduce(f32[16,256]{1,0:T(8,128)S(1)} %fusion.84), channel_id=1, replica_groups=mesh['rows'=32,'cols'=16] {'rows','cols'}, use_global_device_ids=true, to_apply=%region_2.3 | all-reduce | flops 4096 | bytes 32768 | tf_op jit(solution)/shard_map/psum | solution.py:102
  256.7 0.7 stack.4
  257.4 4.5 all-to-all-start
  262.2 0.8 bitcast_subtract_fusion
  263.9 9.6 %all-to-all-done = f32[16,16,256]{2,1,0:T(8,128)S(1)} async-done(((f32[16,16,256]{2,1,0:T(8,128)}), f32[16,16,256]{2,1,0:T(8,128)S(1)}, u32[]{:S(2)}, u32[]{:S(2)}) %all-to-all-start) | async-done | bytes 262176 | tf_op jit(solution)/shard_map/all_to_all | solution.py:119
  273.6 3.0 collective-permute-start.2
  276.6 1.3 collective-permute-start.3
  277.9 1.1 collective-permute-done.2
  279.1 3.8 collective-permute-done.3
  283.0 12.1 %while.22 = (s32[]{:T(128)}, f32[16,2,128]{2,1,0:T(2,128)S(1)}, s32[]{:T(128)}, s32[2]{0:T(128)S(1)}, s32[]{:T(128)}, /*index=5*/f32[3,2,128]{2,0,1:T(4,128)S(1)...) while((s32[]{:T(128)}, f32[16,2,128]{2,1,0:T(2,128)S(1)}, ...), condition=%wide.region_10.11_spmd.clone, body=%wide.region_7.10_spmd.clone.sunk | while | flops 111156288 | bytes 6040561 | solution.py:75
  283.1 0.6 fusion.135
  283.7 1.3 fusion.136
  285.0 0.8 gather_fusion
  285.8 0.7 fusion.138
  286.5 0.6 gather_fusion.2
  287.1 0.6 gather_fusion.1
  287.8 0.6 gather_fusion.3
  288.3 2.1 multiply_reduce_fusion.9
  290.4 4.3 fusion.139
  295.1 15.5 %all_gather.6 = f32[16,4096]{1,0:T(8,128)S(1)} all-gather(f32[16,256]{1,0:T(8,128)S(1)} %bitcast.179), channel_id=1, replica_groups=mesh['rows'=32,'cols'=16] {'cols'}, dimensions={1}, use_global_device_ids=true | all-gather | bytes 278528 | tf_op jit(solution)/shard_map/all_gather | solution.py:138
  310.7 103.5 %all-reduce = (f32[16]{0:T(128)S(1)}, f32[16]{0:T(128)S(1)}) all-reduce(f32[16]{0:T(128)S(1)} %get-tuple-element.325, f32[16]{0:T(128)S(1)} %multiply_reduce_fusion.5), channel_id=1, replica_groups=mesh['rows'=32,'cols'=16] {'rows','cols'}, use_global_device_ids=true, to_apply=%region_4.5 | all-reduce | flops 32 | bytes 256 | tf_op jit(solution)/shard_map/psum | solution.py:105
  414.7 94.7 %psum.53 = f32[16,256]{1,0:T(8,128)S(1)} all-reduce(f32[16,256]{1,0:T(8,128)S(1)} %fusion.82), channel_id=1, replica_groups=mesh['rows'=32,'cols'=16] {'rows','cols'}, use_global_device_ids=true, to_apply=%region_13.14 | all-reduce | flops 4096 | bytes 32768 | tf_op jit(solution)/shard_map/psum | solution.py:102
  509.5 0.5 multiply_reduce_fusion.4
  510.0 0.7 stack.5
  510.8 5.7 all-to-all-start.1
  516.5 97.8 %psum.54 = f32[16]{0:T(128)S(1)} all-reduce(f32[16]{0:T(128)S(1)} %get-tuple-element.327), channel_id=1, replica_groups=mesh['rows'=32,'cols'=16] {'rows','cols'}, use_global_device_ids=true, to_apply=%region_15.16 | all-reduce | flops 16 | bytes 128 | tf_op jit(solution)/shard_map/psum | solution.py:105
  614.5 2.8 collective-permute-start.4
  617.2 1.3 collective-permute-start.5
  618.9 4.0 collective-permute-done.5
  622.9 12.0 %while.23 = (s32[]{:T(128)}, f32[16,2,128]{2,1,0:T(2,128)S(1)}, s32[]{:T(128)}, s32[2]{0:T(128)S(1)}, s32[]{:T(128)}, /*index=5*/f32[3,2,128]{2,0,1:T(4,128)S(1)...) while((s32[]{:T(128)}, f32[16,2,128]{2,1,0:T(2,128)S(1)}, ...), condition=%wide.region_19.20_spmd.clone, body=%wide.region_16.19_spmd.clone.sunk | while | flops 111156288 | bytes 6040561 | solution.py:75
  623.1 0.6 fusion.146
  623.7 1.3 fusion.147
  625.0 0.8 gather_fusion.4
  625.7 0.7 fusion.149
  626.5 0.6 gather_fusion.6
  627.1 0.6 gather_fusion.5
  627.7 0.6 gather_fusion.7
  628.3 2.1 multiply_reduce_fusion.10
  630.4 4.3 fusion.150
  635.0 17.7 %all_gather.7 = f32[16,4096]{1,0:T(8,128)S(1)} all-gather(f32[16,256]{1,0:T(8,128)S(1)} %bitcast.180), channel_id=1, replica_groups=mesh['rows'=32,'cols'=16] {'cols'}, dimensions={1}, use_global_device_ids=true | all-gather | bytes 278528 | tf_op jit(solution)/shard_map/all_gather | solution.py:138
  652.8 107.3 %psum.55 = f32[16]{0:T(128)S(1)} all-reduce(f32[16]{0:T(128)S(1)} %multiply_reduce_fusion.3), channel_id=1, replica_groups=mesh['rows'=32,'cols'=16] {'rows','cols'}, use_global_device_ids=true, to_apply=%region_21.22 | all-reduce | flops 16 | bytes 128 | tf_op jit(solution)/shard_map/psum | solution.py:143
  760.2 0.9 multiply_subtract_fusion
  (70 shorter events, 4.4 us)
Async XLA Ops:
  0.6 255.4 %copy-start = (f32[256,256]{1,0:T(8,128)S(1)}, f32[256,256]{1,0:T(8,128)}, u32[]{:S(2)}) copy-start(f32[256,256]{1,0:T(8,128)} %param.15) | copy-start | bytes 786436
  0.6 8.5 %copy-start.1 = (f32[3,4096]{1,0:T(4,128)S(1)}, f32[3,4096]{1,0:T(4,128)}, u32[]{:S(2)}) copy-start(f32[3,4096]{1,0:T(4,128)} %param.10) | copy-start | bytes 147460
  0.7 8.5 %copy-start.4 = (s32[256]{0:T(256)S(1)}, s32[256]{0:T(256)}, u32[]{:S(2)}) copy-start(s32[256]{0:T(256)} %param.12) | copy-start | bytes 3076
  0.7 130.9 %copy-start.2 = (f32[16,4096]{1,0:T(8,128)S(1)}, f32[16,4096]{1,0:T(8,128)}, u32[]{:S(2)}) copy-start(f32[16,4096]{1,0:T(8,128)} %param.11) | copy-start | bytes 786436
  1.5 276.4 %collective-permute-start = (f32[3,1536]{1,0:T(4,128)S(1)}, f32[3,1536]{1,0:T(4,128)S(1)}, u32[]{:S(2)}, u32[]{:S(2)}) collective-permute-start(f32[3,1536]{1,0:T(4,128)S(1)} %get-tuple-element.318), channel_id=1, source_target_pairs={{0,16},{16,32},{32,48},{48,64},{64,80},{80,96},{96,112},{112,128},... | collective-permute-start | bytes 55304 | tf_op jit(solution)/shard_map/ppermute | solution.py:21
  6.3 271.6 %collective-permute-start.1 = (f32[3,1536]{1,0:T(4,128)S(1)}, f32[3,1536]{1,0:T(4,128)S(1)}, u32[]{:S(2)}, u32[]{:S(2)}) collective-permute-start(f32[3,1536]{1,0:T(4,128)S(1)} %get-tuple-element.319), channel_id=1, source_target_pairs={{16,0},{32,16},{48,32},{64,48},{80,64},{96,80},{112,96},{128,112},... | collective-permute-start | bytes 55304 | tf_op jit(solution)/shard_map/ppermute | solution.py:23
  9.1 252.8 %copy-start.5 = (s32[32]{0:T(128)S(1)}, s32[32]{0:T(128)}, u32[]{:S(2)}) copy-start(s32[32]{0:T(128)} %param.14) | copy-start | bytes 388
  9.1 254.6 %copy-start.3 = (s32[32,18]{0,1:T(8,128)S(1)}, s32[32,18]{0,1:T(8,128)}, u32[]{:S(2)}) copy-start(s32[32,18]{0,1:T(8,128)} %param.13) | copy-start | bytes 6916
  257.4 16.1 %all-to-all-start = ((f32[16,16,256]{2,1,0:T(8,128)}), f32[16,16,256]{2,1,0:T(8,128)S(1)}, u32[]{:S(2)}, u32[]{:S(2)}) async-start(f32[16,16,256]{2,1,0:T(8,128)} %stack.4), calls=%async_computation | async-start | bytes 524288 | tf_op jit(solution)/shard_map/all_to_all | solution.py:119
  273.6 5.5 collective-permute-start.2
  276.6 6.3 collective-permute-start.3
  510.8 103.6 %all-to-all-start.1 = ((f32[16,16,256]{2,1,0:T(8,128)}), f32[16,16,256]{2,1,0:T(8,128)S(1)}, u32[]{:S(2)}, u32[]{:S(2)}) async-start(f32[16,16,256]{2,1,0:T(8,128)} %stack.5), calls=%async_computation.1 | async-start | bytes 524288 | tf_op jit(solution)/shard_map/all_to_all | solution.py:119
  614.5 4.4 collective-permute-start.4
  617.2 5.7 collective-permute-start.5
